TPU v7x, 32 devices: a whole 2x2x4 slice. The times are simulated.
32 devices in a mesh: groups: 2 (over x), sensor: 16 (over z, y, core).
Axes of the slice: x: 2, y: 2, z: 4, core: 2. Of those that a mesh axis runs over, the one named last changes fastest.
Arguments:
- series: float32 [288, 1536], P(None, ('groups', 'sensor')), parts along dimension 1, may hold values from -6 to 6
- starts: int32 [2], P('groups'), parts along dimension 0, may hold values from 0 to 276
- sensor_order: int32 [1536], P(('groups', 'sensor')), parts along dimension 0, may hold values from 0 to 767, each once
- emb_src: float32 [10, 1536], P(None, ('groups', 'sensor')), parts along dimension 1, may hold values from -4.4 to 330
- emb_dst: float32 [10, 1536], P(None, ('groups', 'sensor')), parts along dimension 1, may hold values from -4.4 to 4.4
- start_proj: float32 [2, 32], replicated, may hold values from -4 to 4
- conv_weight: bfloat16 [64, 64], replicated, may hold values from -0.75 to 0.75
- mix_weight: bfloat16 [96, 32], replicated, may hold values from -0.625 to 0.625
- out_grad: bfloat16 [1536, 384], P(('groups', 'sensor')), parts along dimension 0, may hold values from -0.59765625 to 0.59765625
Outputs:
- layer_out: bfloat16 [1536, 384], P(('groups', 'sensor')), parts along dimension 0
- grad_src: float32 [10, 1536], P(None, ('groups', 'sensor')), parts along dimension 1
- grad_dst: float32 [10, 1536], P(None, ('groups', 'sensor')), parts along dimension 1
- grad_mix: float32 [192, 32], P('groups'), parts along dimension 0
There are 2 independent parts, one for each index of `groups`. A program takes and returns all parts, laid end to end along the dimension named above; an argument that names none is the same for every part. Nothing has to cross between parts.
All inputs are finite; a program needn't handle non-finite values.
Results may differ from a plain program's by a relative error of at most 0.035.
Values may be sent and summed in bfloat16 or wider, within the bound.
A program may use at most 64 MiB of HBM per device.

v0:
```python
import math
import jax
import jax.numpy as jnp
from jax import lax
from jax.sharding import PartitionSpec as P

STEPS = 12
highest = lax.Precision.HIGHEST


def front(readings, start_proj, conv_weight):
    sensors_here = readings.shape[0]
    channels = start_proj.shape[1]
    padded = jnp.concatenate(
        [jnp.zeros(readings.shape[:-1] + (1,), jnp.float32), readings], axis=-1
    )
    inputs = (padded[..., None] * start_proj[0] + start_proj[1]).astype(jnp.bfloat16)
    paired = jnp.concatenate([inputs[:, :, :-1, :], inputs[:, :, 1:, :]], axis=-1).reshape(
        -1, 2 * channels
    )
    gate_terms = jnp.dot(paired, conv_weight, preferred_element_type=jnp.float32)
    hidden = (jnp.tanh(gate_terms[:, :channels]) * jax.nn.sigmoid(gate_terms[:, channels:])).astype(
        jnp.bfloat16
    )
    return (hidden.reshape(sensors_here, -1), inputs[:, :, 1:, :].reshape(sensors_here, -1))


def mixing(residual, hidden, diffused, second, mix_weight):
    channels = mix_weight.shape[1]
    stacked = jnp.concatenate(
        [member.reshape(-1, channels) for member in (hidden, diffused, second)], axis=1
    )
    summed = residual.reshape(-1, channels).astype(jnp.float32) + jnp.dot(
        stacked, mix_weight, preferred_element_type=jnp.float32
    )
    return (summed.astype(jnp.bfloat16).reshape(hidden.shape[0], -1), stacked)


def channel_grads(out_grad, mix_weight):
    channels = mix_weight.shape[1]
    row_count = out_grad.shape[0]
    flat_grad = out_grad.reshape(-1, channels)
    dims = (((1,), (1,)), ((), ()))
    grad_once = lax.dot_general(
        flat_grad, mix_weight[channels : 2 * channels], dims, preferred_element_type=jnp.float32
    )
    grad_twice = lax.dot_general(
        flat_grad, mix_weight[2 * channels :], dims, preferred_element_type=jnp.float32
    )
    return (
        grad_once.astype(jnp.bfloat16).reshape(row_count, -1),
        grad_twice.astype(jnp.bfloat16).reshape(row_count, -1),
    )


def tile_probs(rows_emb, cols_emb, row_max, row_total):
    scores = jnp.einsum("ei,ej->ij", rows_emb, cols_emb, precision=highest)
    shares = jnp.exp(jnp.maximum(scores, 0.0) - row_max[:, None]) / row_total[:, None]
    return (scores, shares)


def pair_dot(left, right):
    return lax.dot_general(
        left, right, (((1,), (1,)), ((), ())), preferred_element_type=jnp.float32
    )


def in_blocks(step_fn, status, members, axis_dim):
    amount = members[0].shape[axis_dim]
    span_size = math.gcd(amount, 512)

    def advance(position, current):
        opening = position * span_size
        sliced = tuple(
            (lax.dynamic_slice_in_dim(member, opening, span_size, axis_dim) for member in members)
        )
        return step_fn(current, sliced, opening)

    return lax.fori_loop(0, amount // span_size, advance, status)


def score_grads(status, emb_src, cols_dst, offset, scores, shares, dweights):
    grad_rows, grad_cols = status
    dscore = jnp.where(scores > 0.0, shares * dweights, 0.0)
    grad_rows = grad_rows + jnp.einsum("ej,ij->ei", cols_dst, dscore, precision=highest)
    span_size = dscore.shape[1]
    current = lax.dynamic_slice_in_dim(grad_cols, offset, span_size, 1)
    added = current + jnp.einsum("ei,ij->ej", emb_src, dscore, precision=highest)
    return (grad_rows, lax.dynamic_update_slice_in_dim(grad_cols, added, offset, 1))


def per_device(
    series, starts, sensor_order, emb_src, emb_dst, start_proj, conv_weight, mix_weight, out_grad
):
    local_rows = sensor_order.shape[0]
    embed_dim = emb_src.shape[0]
    channels = start_proj.shape[1]
    all_rows = local_rows * lax.axis_size("sensor")
    windows = jax.vmap(lambda first_step: lax.dynamic_slice_in_dim(series, first_step, STEPS, 0))(
        starts
    )
    flat_windows = windows.reshape(-1, local_rows)
    window_rows = flat_windows.shape[0]

    def pick_step(status, members, offset):
        readings_sum, dst_all = status
        block_windows, block_dst = members
        span_size = block_windows.shape[1]
        onehot = (sensor_order[:, None] == offset + lax.iota(jnp.int32, span_size)[None, :]).astype(
            jnp.float32
        )
        readings_sum = readings_sum + jnp.einsum(
            "wj,pj->wp", block_windows, onehot, precision=highest
        )
        return (readings_sum, lax.dynamic_update_slice_in_dim(dst_all, block_dst, offset, 1))

    readings_sum, dst_all = in_blocks(
        pick_step,
        (
            jnp.zeros((window_rows, local_rows), jnp.float32),
            jnp.zeros((embed_dim, all_rows), jnp.float32),
        ),
        (
            lax.all_gather(flat_windows, "sensor", axis=1, tiled=True),
            lax.all_gather(emb_dst, "sensor", axis=1, tiled=True),
        ),
        1,
    )
    readings = readings_sum.T.reshape(local_rows, -1, STEPS)
    hidden, residual = front(readings, start_proj, conv_weight)
    feat_cols = hidden.shape[1]
    span_all = math.gcd(all_rows, 512)

    def stat_step(position, current):
        best_score, summed = current
        cols_dst = lax.dynamic_slice_in_dim(dst_all, position * span_all, span_all, 1)
        scores = jnp.maximum(jnp.einsum("ei,ej->ij", emb_src, cols_dst, precision=highest), 0.0)
        new_best = jnp.maximum(best_score, jnp.max(scores, axis=1))
        summed = summed * jnp.exp(best_score - new_best) + jnp.sum(
            jnp.exp(scores - new_best[:, None]), axis=1
        )
        return (new_best, summed)

    row_max, row_total = lax.fori_loop(
        0,
        all_rows // span_all,
        stat_step,
        (jnp.zeros((local_rows,), jnp.float32), jnp.zeros((local_rows,), jnp.float32)),
    )
    grad_once, grad_twice = channel_grads(out_grad, mix_weight)

    def spread_step(status, members, offset):
        block_feat = members[0]
        cols_dst = lax.dynamic_slice_in_dim(dst_all, offset, block_feat.shape[0], 1)
        scores, shares = tile_probs(emb_src, cols_dst, row_max, row_total)
        return status + jnp.dot(
            shares.astype(jnp.bfloat16), block_feat, preferred_element_type=jnp.float32
        )

    first_init = jnp.zeros((local_rows, feat_cols), jnp.float32)
    first_result = in_blocks(
        spread_step, first_init, (lax.all_gather(hidden, "sensor", axis=0, tiled=True),), 0
    )
    diffused = first_result.astype(jnp.bfloat16)

    def plain_step(status, members, offset):
        accumulated, grad_rows, grad_cols = status
        return (spread_step(accumulated, members, offset), grad_rows, grad_cols)

    second_init = (
        jnp.zeros((local_rows, feat_cols), jnp.float32),
        jnp.zeros((embed_dim, local_rows), jnp.float32),
        jnp.zeros((embed_dim, all_rows), jnp.float32),
    )
    second_result = in_blocks(
        plain_step, second_init, (lax.all_gather(diffused, "sensor", axis=0, tiled=True),), 0
    )
    second_full, grad_rows, grad_cols = second_result
    second = second_full.astype(jnp.bfloat16)
    layer_out, stacked = mixing(residual, hidden, diffused, second, mix_weight)
    mix_part = lax.dot_general(
        stacked,
        out_grad.reshape(-1, channels),
        (((0,), (0,)), ((), ())),
        preferred_element_type=jnp.float32,
    )
    span_size = math.gcd(lax.axis_size("sensor") * local_rows, 512)

    def piece_term(position):
        cols_dst = lax.dynamic_slice_in_dim(dst_all, position * span_size, span_size, 1)
        scores, shares = tile_probs(emb_src, cols_dst, row_max, row_total)
        return lax.dot_general(
            shares.astype(jnp.bfloat16),
            grad_twice,
            (((0,), (0,)), ((), ())),
            preferred_element_type=jnp.float32,
        )

    adjoint_sum = lax.psum_scatter(
        lax.map(
            piece_term,
            jnp.arange(lax.axis_size("sensor") * local_rows // span_size, dtype=jnp.int32),
        ).reshape(lax.axis_size("sensor") * local_rows, -1),
        "sensor",
        scatter_dimension=0,
        tiled=True,
    )
    carried = (grad_once.astype(jnp.float32) + adjoint_sum).astype(jnp.bfloat16)
    row_delta = jnp.sum(
        grad_twice.astype(jnp.float32) * second_full + carried.astype(jnp.float32) * first_result,
        axis=1,
    )

    def pair_step(status, members, offset):
        block_hidden, block_diff = members
        cols_dst = lax.dynamic_slice_in_dim(dst_all, offset, block_hidden.shape[0], 1)
        scores, shares = tile_probs(emb_src, cols_dst, row_max, row_total)
        dweights = (
            pair_dot(grad_twice, block_diff) + pair_dot(carried, block_hidden) - row_delta[:, None]
        )
        return score_grads(status, emb_src, cols_dst, offset, scores, shares, dweights)

    grad_rows, grad_cols = in_blocks(
        pair_step,
        (grad_rows, grad_cols),
        (
            lax.all_gather(hidden, "sensor", axis=0, tiled=True),
            lax.all_gather(diffused, "sensor", axis=0, tiled=True),
        ),
        0,
    )
    grad_dst = lax.psum_scatter(grad_cols, "sensor", scatter_dimension=1, tiled=True)
    grad_mix = lax.psum(mix_part, "sensor")
    return (layer_out, grad_rows, grad_dst, grad_mix)


def solution(mesh):
    placed = (
        P(None, ("groups", "sensor")),
        P("groups"),
        P(("groups", "sensor")),
        P(None, ("groups", "sensor")),
        P(None, ("groups", "sensor")),
        P(),
        P(),
        P(),
        P(("groups", "sensor"), None),
    )
    return jax.shard_map(
        per_device,
        mesh=mesh,
        in_specs=placed,
        out_specs=(
            P(("groups", "sensor"), None),
            P(None, ("groups", "sensor")),
            P(None, ("groups", "sensor")),
            P("groups", None),
        ),
        check_vma=False,
    )
```

profile of v0, /device:TPU:0, one launch (start us, length us, event | category | flops | bytes accessed | tf_op | source)
XLA Modules:
  0.0 194.4 jit_solution(2964574075094498716)
XLA Ops:
  8.2 23.4 %all-gather = f32[16,48,12]{1,2,0:T(8,128)S(1)} all-gather(f32[1,48,12]{1,2,0:T(8,128)S(1)} %bitcast.98), channel_id=1, replica_groups=mesh['groups'=2,'sensor'=16] {'sensor'}, dimensions={0}, use_global_device_ids=true | all-gather | bytes 39168 | tf_op jit(solution)/shard_map/all_gather | solution.py:124
  31.8 18.0 %all-gather.1 = f32[16,48,10]{1,2,0:T(8,128)S(1)} all-gather(f32[1,48,10]{1,2,0:T(8,128)} %bitcast.100), channel_id=1, replica_groups=mesh['groups'=2,'sensor'=16] {'sensor'}, dimensions={0}, use_global_device_ids=true | all-gather | bytes 32640 | tf_op jit(solution)/shard_map/all_gather | solution.py:125
  50.0 2.7 %while.88 = (s32[]{:T(128)}, f32[12,48]{1,0:T(8,128)S(1)}, f32[10,768]{1,0:T(8,128)S(1)}, f32[12,768]{1,0:T(8,128)S(1)}, s32[48]{0:T(128)}, /*index=5*/f32[10,76...) while((s32[]{:T(128)}, f32[12,48]{1,0:T(8,128)S(1)}, f32[10,768]{1,0:T(8,128)S(1)}, ...), condition=%wide.region_1.0_spmd.clone, body=%wide.region_0.0_spmd.clone.sunk | while | flops 1783175 | bytes 62065 | solution.py:79
  50.0 0.8 convolution_add_fusion.10
  50.9 0.8 convolution_add_fusion.10
  51.9 0.8 convolution_add_fusion.10
  52.7 1.8 while.89
  52.8 0.3 fusion.128
  53.1 0.2 exponential_reduce_fusion.2
  53.4 0.3 fusion.128
  53.7 0.2 exponential_reduce_fusion.2
  53.9 0.3 fusion.128
  54.3 0.2 exponential_reduce_fusion.2
  54.7 0.3 convolution_convert_fusion.1
  55.3 7.5 %while.87 = (s32[]{:T(128)}, f32[3,256,384]{2,1,0:T(8,128)}, s32[3]{0:T(128)S(1)}, f32[10,768]{1,0:T(8,128)S(1)}, f32[10,48]{1,0:T(8,128)S(1)}, /*index=5*/f32[4...) while((s32[]{:T(128)}, f32[3,256,384]{2,1,0:T(8,128)}, ...), condition=%wide.region_11.12_spmd, body=%wide.region_10.11_spmd.sunk | while | flops 10960902 | bytes 505023 | solution.py:200
  55.3 0.6 dynamic_slice.136
  56.5 0.3 fusion.123
  56.8 1.0 fusion.124
  57.8 0.6 dynamic_slice.136
  59.0 0.3 fusion.123
  59.3 1.0 fusion.124
  60.3 0.6 dynamic_slice.136
  61.5 0.3 fusion.123
  61.8 1.0 fusion.124
  62.9 0.6 copy-done.6
  64.2 0.3 copy-done.5
  64.6 0.2 fusion.62
  65.1 20.4 %all_gather.16 = bf16[768,384]{1,0:T(8,128)(2,1)S(1)} all-gather(bf16[48,384]{1,0:T(8,128)(2,1)S(1)} %reshape.86), channel_id=1, replica_groups=mesh['groups'=2,'sensor'=16] {'sensor'}, dimensions={0}, use_global_device_ids=true | all-gather | bytes 626688 | tf_op jit(solution)/shard_map/all_gather | solution.py:162
  85.5 1.4 while.90
  85.5 0.3 fusion.135
  85.8 0.2 convolution_add_fusion.11
  86.0 0.3 fusion.135
  86.2 0.2 convolution_add_fusion.11
  86.4 0.3 fusion.135
  86.7 0.2 convolution_add_fusion.11
  86.9 0.3 fusion.49
  87.7 20.1 %all_gather.17 = bf16[768,384]{1,0:T(8,128)(2,1)S(1)} all-gather(bf16[48,384]{1,0:T(8,128)(2,1)S(1)} %convert_element_type.68), channel_id=1, replica_groups=mesh['groups'=2,'sensor'=16] {'sensor'}, dimensions={0}, use_global_device_ids=true | all-gather | bytes 626688 | tf_op jit(solution)/shard_map/all_gather | solution.py:176
  107.9 1.4 while.91
  107.9 0.3 fusion.140
  108.1 0.2 convolution_add_fusion.12
  108.3 0.3 fusion.140
  108.6 0.2 convolution_add_fusion.12
  108.8 0.3 fusion.140
  109.1 0.2 convolution_add_fusion.12
  109.2 12.6 %reduce-scatter.5.cloned.1.call-done = f32[48,384]{1,0:T(8,128)} async-done(((f32[768,384]{1,0:T(8,128)}), f32[48,384]{1,0:T(8,128)}) %reduce-scatter.5.cloned.1.call-update) | async-done | bytes 73744 | tf_op jit(solution)/shard_map/reduce_scatter | solution.py:199
  121.9 1.0 add_reduce_fusion
  123.2 3.0 %while.92 = (s32[]{:T(128)}, f32[10,48]{1,0:T(8,128)S(1)}, f32[10,768]{1,0:T(8,128)S(1)}, f32[10,768]{1,0:T(8,128)S(1)}, f32[10,48]{1,0:T(8,128)S(1)}, /*index=5...) while((s32[]{:T(128)}, f32[10,48]{1,0:T(8,128)S(1)}, ...), condition=%wide.region_15.16_spmd.clone, body=%wide.region_14.15_spmd.clone.sunk | while | flops 23399876 | bytes 904809 | solution.py:79
  123.2 0.2 fusion.151
  123.4 0.2 fusion.152
  123.7 0.2 fusion.153
  124.2 0.2 fusion.151
  124.4 0.2 fusion.152
  124.7 0.2 fusion.153
  125.0 0.2 fusion.154
  125.2 0.2 fusion.151
  125.4 0.2 fusion.152
  125.7 0.2 fusion.153
  126.0 0.2 fusion.154
  126.2 0.9 copy.46
  127.2 0.2 fusion.55
  127.4 0.2 fusion.48
  127.7 0.8 reshape.89
  128.5 57.7 %psum.7 = f32[96,32]{0,1:T(8,128)} all-reduce(f32[96,32]{0,1:T(8,128)S(1)} %fusion.55), channel_id=1, replica_groups=mesh['groups'=2,'sensor'=16] {'sensor'}, use_global_device_ids=true, to_apply=%region_17.18 | all-reduce | flops 3072 | bytes 24576 | tf_op jit(solution)/shard_map/psum | solution.py:233
  186.1 1.4 copy.47
  (75 shorter events, 4.0 us)
Async XLA Ops:
  7.2 0.9 copy-start
  7.2 45.6 %copy-start.1 = (f32[10,48]{1,0:T(8,128)S(1)}, f32[10,48]{1,0:T(8,128)}, u32[]{:S(2)}) copy-start(f32[10,48]{1,0:T(8,128)} %param.24) | copy-start | bytes 5764
  7.2 114.7 %reduce-scatter.5.cloned.1.call-start = ((), (), s32[]{:S(2)}) async-start(), calls=%async_computation.2 | async-start | bytes 1253376 | tf_op jit(solution)/shard_map/reduce_scatter | solution.py:199
  31.7 22.8 %copy-start.3 = (bf16[48,384]{1,0:T(8,128)(2,1)S(1)}, bf16[48,384]{1,0:T(8,128)(2,1)}, u32[]{:S(2)}) copy-start(bf16[48,384]{1,0:T(8,128)(2,1)} %param.29) | copy-start | bytes 110596
  31.8 22.9 %copy-start.4 = (bf16[96,32]{0,1:T(8,128)(2,1)S(1)}, bf16[96,32]{0,1:T(8,128)(2,1)}, u32[]{:S(2)}) copy-start(bf16[96,32]{0,1:T(8,128)(2,1)} %param.28) | copy-start | bytes 18436
  62.8 0.7 copy-start.6
  62.8 123.3 %reduce-scatter.7.cloned.1.call-start = ((), (), s32[]{:S(2)}) async-start(), calls=%async_computation.3 | async-start | bytes 417792
  63.8 0.7 copy-start.5
  126.2 61.3 %copy-start.2 = (f32[10,48]{1,0:T(8,128)}, f32[10,48]{1,0:T(8,128)S(1)}, u32[]{:S(2)}) copy-start(f32[10,48]{1,0:T(8,128)S(1)} %get-tuple-element.696) | copy-start | bytes 5764
Sparse Core Ops, SparseCore 0:
  62.9 58.8 reduce-scatter.4
  127.3 54.7 reduce-scatter.6
where the time goes:
time: 195 us; the launch traced here: 194 us
  blocking collectives  140 us (72%)
  between operations  15 us (8%)
  matrix products  13.9 us (7%)
  waiting for transfers between devices  12.7 us (7%)
  local copies, waits for them, and re-layouts  8.47 us (4%)
  loops' own time  2.58 us (1%)
  other arithmetic  2.1 us (1%)
    psum x1, blocking collectives, per_device(): grad_mix = lax.psum(mix_part, 'sensor')  57.7 us
    all_gather x1, blocking collectives, per_device(): lax.all_gather(flat_windows, 'sensor', axis=1, tiled=True)  23.4 us
    all_gather x1, blocking collectives, per_device(): lax.all_gather(hidden, 'sensor', axis=0, tiled=True)  20.4 us
    all_gather x1, blocking collectives, per_device(): lax.all_gather(diffused, 'sensor', axis=0, tiled=True)  20.1 us
    all_gather x1, blocking collectives, per_device(): lax.all_gather(emb_dst, 'sensor', axis=1, tiled=True)  18 us
    reduce_scatter x1, waiting for transfers between devices, per_device(): lax.psum_scatter(lax.map(piece_term, jnp.arange(lax.axis_size('sensor') *...  12.6 us
  transfers between devices with their start and end apart: 2, of which 1 were waited for; matrix products, arithmetic and copies ran while one was open for 3% of the time, Pallas kernels for 0%

commit v1 on v0

--- a/solution.py
+++ b/solution.py
@@ -6,6 +6,22 @@
 
 STEPS = 12
 highest = lax.Precision.HIGHEST
+
+
+def collect(x, axis, dim):
+    ways, here, step = (lax.axis_size(axis), lax.axis_index(axis), x.shape[dim])
+    shape = [n * ways if d == dim else n for d, n in enumerate(x.shape)]
+    full = lax.dynamic_update_slice_in_dim(jnp.zeros(shape, x.dtype), x, here * step, axis=dim)
+    going_up = going_down = x
+    for far in range(1, ways // 2 + 1):
+        going_up = lax.ppermute(going_up, axis, [(d, (d + 1) % ways) for d in range(ways)])
+        full = lax.dynamic_update_slice_in_dim(full, going_up, (here - far) % ways * step, axis=dim)
+        if 2 * far < ways:
+            going_down = lax.ppermute(going_down, axis, [(d, (d - 1) % ways) for d in range(ways)])
+            full = lax.dynamic_update_slice_in_dim(
+                full, going_down, (here + far) % ways * step, axis=dim
+            )
+    return full
 
 
 def front(readings, start_proj, conv_weight):
@@ -120,10 +136,7 @@
             jnp.zeros((window_rows, local_rows), jnp.float32),
             jnp.zeros((embed_dim, all_rows), jnp.float32),
         ),
-        (
-            lax.all_gather(flat_windows, "sensor", axis=1, tiled=True),
-            lax.all_gather(emb_dst, "sensor", axis=1, tiled=True),
-        ),
+        (collect(flat_windows, "sensor", 1), lax.all_gather(emb_dst, "sensor", axis=1, tiled=True)),
         1,
     )
     readings = readings_sum.T.reshape(local_rows, -1, STEPS)

time: 195 us -> 217 us (1.11)
  starting transfers between devices: 0.08 us -> 28.1 us
  blocking collectives: 140 us -> 118 us
  waiting for transfers between devices: 12.7 us -> 22.9 us
  local copies, waits for them, and re-layouts: 8.47 us -> 14.2 us
    ppermute x0 -> x15, starting transfers between devices: none -> 28 us  [the longest x7 27.1 us: collect(): lax.ppermute(going_down, axis, [(d, (d - 1) % ways) for d in range(ways)])]
    all_gather x1 -> x0, blocking collectives: 23.4 us -> none  [per_device(): lax.all_gather(flat_windows, 'sensor', axis=1, tiled=True)]
    ppermute x0 -> x15, waiting for transfers between devices: none -> 6.51 us  [the longest x7 6.05 us: collect(): lax.ppermute(going_down, axis, [(d, (d - 1) % ways) for d in range(ways)])]
    dynamic_update_slice x0 -> x16, local copies, waits for them, and re-layouts: none -> 4.95 us  [the longest x8 2.4 us: collect(): lax.dynamic_update_slice_in_dim(full, going_up, (here - far) % ways * ste...]
    reduce_scatter x1, waiting for transfers between devices: 12.6 us -> 16.3 us  [per_device(): lax.psum_scatter(lax.map(piece_term, jnp.arange(lax.axis_size('sensor') *...]
  transfers between devices with their start and end apart: 2 -> 17, of which waited for: 1 -> 12; matrix products, arithmetic and copies ran while one was open for 3% -> 7% of each run, Pallas kernels for 0% -> 0%
where the time goes in v1:
time: 217 us
  blocking collectives  118 us (54%)
  starting transfers between devices  28.1 us (13%)
  waiting for transfers between devices  22.9 us (11%)
  between operations  15.1 us (7%)
  local copies, waits for them, and re-layouts  14.2 us (7%)
  matrix products  13.3 us (6%)
  loops' own time  2.51 us (1%)
    psum x1, blocking collectives, per_device(): grad_mix = lax.psum(mix_part, 'sensor')  57.7 us
    ppermute x7, starting transfers between devices, collect(): lax.ppermute(going_down, axis, [(d, (d - 1) % ways) for d in range(ways)])  27.1 us
    all_gather x1, blocking collectives, per_device(): lax.all_gather(diffused, 'sensor', axis=0, tiled=True)  21.1 us
    all_gather x1, blocking collectives, per_device(): lax.all_gather(emb_dst, 'sensor', axis=1, tiled=True)  19.9 us
    all_gather x1, blocking collectives, per_device(): lax.all_gather(hidden, 'sensor', axis=0, tiled=True)  19.6 us
    reduce_scatter x1, waiting for transfers between devices, per_device(): lax.psum_scatter(lax.map(piece_term, jnp.arange(lax.axis_size('sensor') *...  16.3 us
    ppermute x7, waiting for transfers between devices, collect(): lax.ppermute(going_down, axis, [(d, (d - 1) % ways) for d in range(ways)])  6.05 us
  transfers between devices with their start and end apart: 17, of which 12 were waited for; matrix products, arithmetic and copies ran while one was open for 7% of the time, Pallas kernels for 0%

profile of v1, /device:TPU:0, one launch (start us, length us, event | category | flops | bytes accessed | tf_op | source)
XLA Modules:
  0.0 216.5 jit_solution(15011983800272006375)
XLA Ops:
  8.2 0.5 collective-permute-start
  8.7 5.0 %collective-permute-start.1 = (f32[12,48]{1,0:T(8,128)S(1)}, f32[12,48]{1,0:T(8,128)S(1)}, u32[]{:S(2)}, u32[]{:S(2)}) collective-permute-start(f32[12,48]{1,0:T(8,128)S(1)} %copy.47), channel_id=1, source_target_pairs={{0,15},{1,0},{2,1},{3,2},{4,3},{5,4},{6,5},{7,6},{8,7},{9,8},{10,9... | collective-permute-start | bytes 6920 | tf_op jit(solution)/shard_map/ppermute | solution.py:20
  13.7 0.9 reshape.90
  14.6 1.0 convolution_convert_fusion.1
  15.6 1.0 fusion.49
  16.6 0.8 slice_bitcast_fusion.1
  17.3 19.9 %all-gather = f32[16,48,10]{1,2,0:T(8,128)S(1)} all-gather(f32[1,48,10]{1,2,0:T(8,128)} %bitcast.92), channel_id=1, replica_groups=mesh['groups'=2,'sensor'=16] {'sensor'}, dimensions={0}, use_global_device_ids=true | all-gather | bytes 32640 | tf_op jit(solution)/shard_map/all_gather | solution.py:139
  37.3 0.5 collective-permute-start.4
  37.8 0.9 collective-permute-done.3
  38.7 4.4 %collective-permute-start.5 = (f32[12,48]{1,0:T(8,128)S(1)}, f32[12,48]{1,0:T(8,128)S(1)}, u32[]{:S(2)}, u32[]{:S(2)}) collective-permute-start(f32[12,48]{1,0:T(8,128)S(1)} %collective-permute-done.3), channel_id=1, source_target_pairs={{0,15},{1,0},{2,1},{3,2},{4,3},{5,4},{6,5},{7,6},{8,7},{9,8},{10,9... | collective-permute-start | bytes 6920 | tf_op jit(solution)/shard_map/ppermute | solution.py:20
  43.1 1.3 collective-permute-done.5
  44.4 4.4 %collective-permute-start.7 = (f32[12,48]{1,0:T(8,128)S(1)}, f32[12,48]{1,0:T(8,128)S(1)}, u32[]{:S(2)}, u32[]{:S(2)}) collective-permute-start(f32[12,48]{1,0:T(8,128)S(1)} %collective-permute-done.5), channel_id=1, source_target_pairs={{0,15},{1,0},{2,1},{3,2},{4,3},{5,4},{6,5},{7,6},{8,7},{9,8},{10,9... | collective-permute-start | bytes 6920 | tf_op jit(solution)/shard_map/ppermute | solution.py:20
  48.9 1.3 collective-permute-done.7
  50.2 4.4 %collective-permute-start.9 = (f32[12,48]{1,0:T(8,128)S(1)}, f32[12,48]{1,0:T(8,128)S(1)}, u32[]{:S(2)}, u32[]{:S(2)}) collective-permute-start(f32[12,48]{1,0:T(8,128)S(1)} %collective-permute-done.7), channel_id=1, source_target_pairs={{0,15},{1,0},{2,1},{3,2},{4,3},{5,4},{6,5},{7,6},{8,7},{9,8},{10,9... | collective-permute-start | bytes 6920 | tf_op jit(solution)/shard_map/ppermute | solution.py:20
  54.7 1.3 collective-permute-done.9
  56.0 4.4 %collective-permute-start.11 = (f32[12,48]{1,0:T(8,128)S(1)}, f32[12,48]{1,0:T(8,128)S(1)}, u32[]{:S(2)}, u32[]{:S(2)}) collective-permute-start(f32[12,48]{1,0:T(8,128)S(1)} %collective-permute-done.9), channel_id=1, source_target_pairs={{0,15},{1,0},{2,1},{3,2},{4,3},{5,4},{6,5},{7,6},{8,7},{9,8},{10,9... | collective-permute-start | bytes 6920 | tf_op jit(solution)/shard_map/ppermute | solution.py:20
  60.5 1.3 collective-permute-done.11
  61.8 4.4 %collective-permute-start.13 = (f32[12,48]{1,0:T(8,128)S(1)}, f32[12,48]{1,0:T(8,128)S(1)}, u32[]{:S(2)}, u32[]{:S(2)}) collective-permute-start(f32[12,48]{1,0:T(8,128)S(1)} %collective-permute-done.11), channel_id=1, source_target_pairs={{0,15},{1,0},{2,1},{3,2},{4,3},{5,4},{6,5},{7,6},{8,7},{9,8},{10,9... | collective-permute-start | bytes 6920 | tf_op jit(solution)/shard_map/ppermute | solution.py:20
  67.0 0.3 dynamic_update_slice.66
  67.4 0.3 dynamic_update_slice.67
  67.7 0.3 dynamic_update_slice.68
  68.0 0.3 dynamic_update_slice.69
  68.2 0.3 dynamic_update_slice.70
  68.5 0.3 dynamic_update_slice.71
  68.9 0.3 dynamic_update_slice.72
  69.2 0.3 dynamic_update_slice.73
  69.5 0.3 dynamic_update_slice.74
  69.9 0.3 dynamic_update_slice.75
  70.2 0.3 dynamic_update_slice.76
  70.5 0.3 dynamic_update_slice.77
  70.9 0.3 dynamic_update_slice.78
  71.2 0.3 dynamic_update_slice.79
  71.5 0.3 dynamic_update_slice.80
  72.2 0.8 while.88
  73.0 1.8 while.89
  73.0 0.3 fusion.128
  73.6 0.3 fusion.128
  74.2 0.3 fusion.128
  74.8 7.5 %while.87 = (s32[]{:T(128)}, f32[3,256,384]{2,1,0:T(8,128)}, s32[3]{0:T(128)S(1)}, f32[10,768]{1,0:T(8,128)S(1)}, f32[10,48]{1,0:T(8,128)S(1)}, /*index=5*/f32[4...) while((s32[]{:T(128)}, f32[3,256,384]{2,1,0:T(8,128)}, ...), condition=%wide.region_11.12_spmd, body=%wide.region_10.11_spmd.sunk | while | flops 10960902 | bytes 505523 | solution.py:213
  74.8 0.6 dynamic_slice.136
  76.0 0.3 fusion.123
  76.3 1.0 fusion.124
  77.3 0.6 dynamic_slice.136
  78.5 0.3 fusion.123
  78.8 1.0 fusion.124
  79.7 0.6 dynamic_slice.136
  81.2 1.0 fusion.124
  83.7 19.6 %all_gather.12 = bf16[768,384]{1,0:T(8,128)(2,1)S(1)} all-gather(bf16[48,384]{1,0:T(8,128)(2,1)S(1)} %reshape.86), channel_id=1, replica_groups=mesh['groups'=2,'sensor'=16] {'sensor'}, dimensions={0}, use_global_device_ids=true | all-gather | bytes 626688 | tf_op jit(solution)/shard_map/all_gather | solution.py:175
  103.3 1.4 while.90
  103.8 0.3 fusion.135
  104.3 0.3 fusion.135
  105.2 21.1 %all_gather.13 = bf16[768,384]{1,0:T(8,128)(2,1)S(1)} all-gather(bf16[48,384]{1,0:T(8,128)(2,1)S(1)} %convert_element_type.68), channel_id=1, replica_groups=mesh['groups'=2,'sensor'=16] {'sensor'}, dimensions={0}, use_global_device_ids=true | all-gather | bytes 626688 | tf_op jit(solution)/shard_map/all_gather | solution.py:189
  126.3 1.4 while.91
  126.8 0.3 fusion.140
  127.3 0.3 fusion.140
  127.7 16.3 %reduce-scatter.5.cloned.1.call-done = f32[48,384]{1,0:T(8,128)} async-done(((f32[768,384]{1,0:T(8,128)}), f32[48,384]{1,0:T(8,128)}) %reduce-scatter.5.cloned.1.call-update) | async-done | bytes 73744 | tf_op jit(solution)/shard_map/reduce_scatter | solution.py:212
  144.0 1.0 add_reduce_fusion
  145.3 3.0 %while.92 = (s32[]{:T(128)}, f32[10,48]{1,0:T(8,128)S(1)}, f32[10,768]{1,0:T(8,128)S(1)}, f32[10,768]{1,0:T(8,128)S(1)}, f32[10,48]{1,0:T(8,128)S(1)}, /*index=5...) while((s32[]{:T(128)}, f32[10,48]{1,0:T(8,128)S(1)}, ...), condition=%wide.region_15.16_spmd.clone, body=%wide.region_14.15_spmd.clone.sunk | while | flops 23399876 | bytes 904801 | solution.py:95
  146.3 0.3 fusion.152
  147.3 0.3 fusion.152
  148.3 0.9 copy.45
  149.8 0.8 reshape.89
  150.6 57.7 %psum.7 = f32[96,32]{0,1:T(8,128)} all-reduce(f32[96,32]{0,1:T(8,128)S(1)} %fusion.55), channel_id=1, replica_groups=mesh['groups'=2,'sensor'=16] {'sensor'}, use_global_device_ids=true, to_apply=%region_17.18 | all-reduce | flops 3072 | bytes 24576 | tf_op jit(solution)/shard_map/psum | solution.py:246
  208.3 1.4 copy.46
  (117 shorter events, 9.8 us)
Async XLA Ops:
  7.2 0.9 copy-start
  7.2 136.8 %reduce-scatter.5.cloned.1.call-start = ((), (), s32[]{:S(2)}) async-start(), calls=%async_computation.2 | async-start | bytes 1253376 | tf_op jit(solution)/shard_map/reduce_scatter | solution.py:212
  8.2 9.1 %collective-permute-start = (f32[12,48]{1,0:T(8,128)S(1)}, f32[12,48]{1,0:T(8,128)S(1)}, u32[]{:S(2)}, u32[]{:S(2)}) collective-permute-start(f32[12,48]{1,0:T(8,128)S(1)} %copy.47), channel_id=1, source_target_pairs={{0,1},{1,2},{2,3},{3,4},{4,5},{5,6},{6,7},{7,8},{8,9},{9,10},{10,1... | collective-permute-start | bytes 6920 | tf_op jit(solution)/shard_map/ppermute | solution.py:17
  8.7 28.6 %collective-permute-start.1 = (f32[12,48]{1,0:T(8,128)S(1)}, f32[12,48]{1,0:T(8,128)S(1)}, u32[]{:S(2)}, u32[]{:S(2)}) collective-permute-start(f32[12,48]{1,0:T(8,128)S(1)} %copy.47), channel_id=1, source_target_pairs={{0,15},{1,0},{2,1},{3,2},{4,3},{5,4},{6,5},{7,6},{8,7},{9,8},{10,9... | collective-permute-start | bytes 6920 | tf_op jit(solution)/shard_map/ppermute | solution.py:20
  17.3 20.0 %collective-permute-start.2 = (f32[12,48]{1,0:T(8,128)S(1)}, f32[12,48]{1,0:T(8,128)S(1)}, u32[]{:S(2)}, u32[]{:S(2)}) collective-permute-start(f32[12,48]{1,0:T(8,128)S(1)} %collective-permute-done), channel_id=1, source_target_pairs={{0,1},{1,2},{2,3},{3,4},{4,5},{5,6},{6,7},{7,8},{8,9},{9,10},{10,1... | collective-permute-start | bytes 6920 | tf_op jit(solution)/shard_map/ppermute | solution.py:17
  37.3 34.9 %copy-start.5 = (s32[48]{0:T(128)S(1)}, s32[48]{0:T(128)}, u32[]{:S(2)}) copy-start(s32[48]{0:T(128)} %param.23) | copy-start | bytes 580
  37.3 1.4 collective-permute-start.3
  37.3 5.8 %collective-permute-start.4 = (f32[12,48]{1,0:T(8,128)S(1)}, f32[12,48]{1,0:T(8,128)S(1)}, u32[]{:S(2)}, u32[]{:S(2)}) collective-permute-start(f32[12,48]{1,0:T(8,128)S(1)} %collective-permute-done.2), channel_id=1, source_target_pairs={{0,1},{1,2},{2,3},{3,4},{4,5},{5,6},{6,7},{7,8},{8,9},{9,10},{10,1... | collective-permute-start | bytes 6920 | tf_op jit(solution)/shard_map/ppermute | solution.py:17
  38.7 5.8 %collective-permute-start.5 = (f32[12,48]{1,0:T(8,128)S(1)}, f32[12,48]{1,0:T(8,128)S(1)}, u32[]{:S(2)}, u32[]{:S(2)}) collective-permute-start(f32[12,48]{1,0:T(8,128)S(1)} %collective-permute-done.3), channel_id=1, source_target_pairs={{0,15},{1,0},{2,1},{3,2},{4,3},{5,4},{6,5},{7,6},{8,7},{9,8},{10,9... | collective-permute-start | bytes 6920 | tf_op jit(solution)/shard_map/ppermute | solution.py:20
  43.1 5.8 %collective-permute-start.6 = (f32[12,48]{1,0:T(8,128)S(1)}, f32[12,48]{1,0:T(8,128)S(1)}, u32[]{:S(2)}, u32[]{:S(2)}) collective-permute-start(f32[12,48]{1,0:T(8,128)S(1)} %collective-permute-done.4), channel_id=1, source_target_pairs={{0,1},{1,2},{2,3},{3,4},{4,5},{5,6},{6,7},{7,8},{8,9},{9,10},{10,1... | collective-permute-start | bytes 6920 | tf_op jit(solution)/shard_map/ppermute | solution.py:17
  44.4 5.8 %collective-permute-start.7 = (f32[12,48]{1,0:T(8,128)S(1)}, f32[12,48]{1,0:T(8,128)S(1)}, u32[]{:S(2)}, u32[]{:S(2)}) collective-permute-start(f32[12,48]{1,0:T(8,128)S(1)} %collective-permute-done.5), channel_id=1, source_target_pairs={{0,15},{1,0},{2,1},{3,2},{4,3},{5,4},{6,5},{7,6},{8,7},{9,8},{10,9... | collective-permute-start | bytes 6920 | tf_op jit(solution)/shard_map/ppermute | solution.py:20
  48.9 5.8 %collective-permute-start.8 = (f32[12,48]{1,0:T(8,128)S(1)}, f32[12,48]{1,0:T(8,128)S(1)}, u32[]{:S(2)}, u32[]{:S(2)}) collective-permute-start(f32[12,48]{1,0:T(8,128)S(1)} %collective-permute-done.6), channel_id=1, source_target_pairs={{0,1},{1,2},{2,3},{3,4},{4,5},{5,6},{6,7},{7,8},{8,9},{9,10},{10,1... | collective-permute-start | bytes 6920 | tf_op jit(solution)/shard_map/ppermute | solution.py:17
  50.2 5.8 %collective-permute-start.9 = (f32[12,48]{1,0:T(8,128)S(1)}, f32[12,48]{1,0:T(8,128)S(1)}, u32[]{:S(2)}, u32[]{:S(2)}) collective-permute-start(f32[12,48]{1,0:T(8,128)S(1)} %collective-permute-done.7), channel_id=1, source_target_pairs={{0,15},{1,0},{2,1},{3,2},{4,3},{5,4},{6,5},{7,6},{8,7},{9,8},{10,9... | collective-permute-start | bytes 6920 | tf_op jit(solution)/shard_map/ppermute | solution.py:20
  54.7 5.8 %collective-permute-start.10 = (f32[12,48]{1,0:T(8,128)S(1)}, f32[12,48]{1,0:T(8,128)S(1)}, u32[]{:S(2)}, u32[]{:S(2)}) collective-permute-start(f32[12,48]{1,0:T(8,128)S(1)} %collective-permute-done.8), channel_id=1, source_target_pairs={{0,1},{1,2},{2,3},{3,4},{4,5},{5,6},{6,7},{7,8},{8,9},{9,10},{10,1... | collective-permute-start | bytes 6920 | tf_op jit(solution)/shard_map/ppermute | solution.py:17
  56.0 5.8 %collective-permute-start.11 = (f32[12,48]{1,0:T(8,128)S(1)}, f32[12,48]{1,0:T(8,128)S(1)}, u32[]{:S(2)}, u32[]{:S(2)}) collective-permute-start(f32[12,48]{1,0:T(8,128)S(1)} %collective-permute-done.9), channel_id=1, source_target_pairs={{0,15},{1,0},{2,1},{3,2},{4,3},{5,4},{6,5},{7,6},{8,7},{9,8},{10,9... | collective-permute-start | bytes 6920 | tf_op jit(solution)/shard_map/ppermute | solution.py:20
  60.5 5.8 %collective-permute-start.12 = (f32[12,48]{1,0:T(8,128)S(1)}, f32[12,48]{1,0:T(8,128)S(1)}, u32[]{:S(2)}, u32[]{:S(2)}) collective-permute-start(f32[12,48]{1,0:T(8,128)S(1)} %collective-permute-done.10), channel_id=1, source_target_pairs={{0,1},{1,2},{2,3},{3,4},{4,5},{5,6},{6,7},{7,8},{8,9},{9,10},{10,1... | collective-permute-start | bytes 6920 | tf_op jit(solution)/shard_map/ppermute | solution.py:17
  61.8 9.8 %collective-permute-start.13 = (f32[12,48]{1,0:T(8,128)S(1)}, f32[12,48]{1,0:T(8,128)S(1)}, u32[]{:S(2)}, u32[]{:S(2)}) collective-permute-start(f32[12,48]{1,0:T(8,128)S(1)} %collective-permute-done.11), channel_id=1, source_target_pairs={{0,15},{1,0},{2,1},{3,2},{4,3},{5,4},{6,5},{7,6},{8,7},{9,8},{10,9... | collective-permute-start | bytes 6920 | tf_op jit(solution)/shard_map/ppermute | solution.py:20
  66.2 5.8 %collective-permute-start.14 = (f32[12,48]{1,0:T(8,128)S(1)}, f32[12,48]{1,0:T(8,128)S(1)}, u32[]{:S(2)}, u32[]{:S(2)}) collective-permute-start(f32[12,48]{1,0:T(8,128)S(1)} %collective-permute-done.12), channel_id=1, source_target_pairs={{0,1},{1,2},{2,3},{3,4},{4,5},{5,6},{6,7},{7,8},{8,9},{9,10},{10,1... | collective-permute-start | bytes 6920 | tf_op jit(solution)/shard_map/ppermute | solution.py:17
  66.3 6.7 %copy-start.1 = (f32[10,48]{1,0:T(8,128)S(1)}, f32[10,48]{1,0:T(8,128)}, u32[]{:S(2)}) copy-start(f32[10,48]{1,0:T(8,128)} %param.24) | copy-start | bytes 5764
  82.3 126.0 %reduce-scatter.7.cloned.1.call-start = ((), (), s32[]{:S(2)}) async-start(), calls=%async_computation.3 | async-start | bytes 417792
  82.4 0.7 copy-start.4
  148.3 61.4 %copy-start.2 = (f32[10,48]{1,0:T(8,128)}, f32[10,48]{1,0:T(8,128)S(1)}, u32[]{:S(2)}) copy-start(f32[10,48]{1,0:T(8,128)S(1)} %get-tuple-element.696) | copy-start | bytes 5764
  148.3 1.2 copy-start.3
Sparse Core Ops, SparseCore 0:
  82.4 61.5 reduce-scatter.4
  149.4 54.6 reduce-scatter.6
